TPU v7x, 32 devices: a whole 2x2x4 slice. The times are simulated.
32 devices in a mesh: batch: 4 (over y, core), seq: 8 (over z, x).
Axes of the slice: x: 2, y: 2, z: 4, core: 2. Of those that a mesh axis runs over, the one named last changes fastest.
Arguments:
- tokens: bfloat16 [4, 1024, 1024], P('batch', 'seq'), may hold values from -6 to 6
- w_query: bfloat16 [512, 512], replicated, may hold values from -0.25 to 0.25
- w_value: bfloat16 [512, 512], replicated, may hold values from -0.25 to 0.25
- w_out: bfloat16 [512, 512], replicated, may hold values from -0.25 to 0.25
- long_filter: float32 [512, 1024], P('seq'), may hold values from -0.1875 to 0.1875
- cotangent: bfloat16 [4, 1024, 1024], P('batch', 'seq'), may hold values from -6 to 6
Outputs:
- block_out: bfloat16 [4, 1024, 1024], P('batch', 'seq')
- grad_tokens: bfloat16 [4, 1024, 1024], P('batch', 'seq')
- grad_query: float32 [512, 512], P('seq')
- grad_value: float32 [512, 512], P('seq')
- grad_out: float32 [512, 512], P('seq')
- grad_filter: float32 [512, 1024], P('seq')
All inputs are finite; a program needn't handle non-finite values.
Results may differ from a plain program's by a relative error of at most 0.017.
Values may be sent and summed in bfloat16 or wider, within the bound.
A program may use at most 64 MiB of HBM per device.

v0:
```python
import math
import jax
import jax.numpy as jnp
from jax import lax
from jax.sharding import PartitionSpec as P

precise = lax.Precision.HIGH


def swapped(x, axis, stride):
    return lax.ppermute(x, axis, [(i, i ^ 1 << stride) for i in range(lax.axis_size(axis))])


def angle_tables(count_rows, count_cols, period):
    left = lax.broadcasted_iota(jnp.int32, (count_rows, count_cols), 0)
    right = lax.broadcasted_iota(jnp.int32, (count_rows, count_cols), 1)
    turns = left * right % period
    angle = turns.astype(jnp.float32) * (2.0 * math.pi / period)
    return (jnp.cos(angle), jnp.sin(angle))


def rotation(cosines, sines, direction):
    upper = jnp.stack([cosines, direction * sines])
    lower_row = jnp.stack([-direction * sines, cosines])
    return jnp.stack([upper, lower_row])


def split_sizes(length):
    period = 2 * length
    first = 1 << (period.bit_length() - 1 + 1) // 2
    return (first, period // first)


def make_tables(first, second):
    cos_first, sin_first = angle_tables(first, first, first)
    cos_twist, sin_twist = angle_tables(first, second, first * second)
    cos_second, sin_second = angle_tables(second, second, second)
    forward_first = rotation(cos_first, sin_first, 1.0)
    inverse_first = rotation(cos_first, sin_first, -1.0)
    forward_second = rotation(cos_second, sin_second, 1.0)
    inverse_second = rotation(cos_second, sin_second, -1.0)
    return (forward_first, inverse_first, forward_second, inverse_second, cos_twist, sin_twist)


def forward_spectrum(signal, tables, first, second):
    forward_first, inverse_first, forward_second, inverse_second, cos_twist, sin_twist = tables
    lower = first // 2
    folded = signal.reshape(2, signal.shape[1], lower, second)
    section = jnp.einsum("brnm,abnk->arkm", folded, forward_first[:, :, :lower], precision=precise)
    turned = jnp.stack(
        [
            section[0] * cos_twist + section[1] * sin_twist,
            section[1] * cos_twist - section[0] * sin_twist,
        ]
    )
    return jnp.einsum("brkm,abmj->arkj", turned, forward_second, precision=precise)


def inverse_spectrum(spectrum, tables, first, second, both):
    forward_first, inverse_first, forward_second, inverse_second, cos_twist, sin_twist = tables
    lower = first // 2
    rows = spectrum.shape[1]
    inner = jnp.einsum("brkj,abjm->arkm", spectrum, inverse_second, precision=precise)
    turned = jnp.stack(
        [inner[0] * cos_twist - inner[1] * sin_twist, inner[1] * cos_twist + inner[0] * sin_twist]
    )
    if both:
        signal = jnp.einsum(
            "brkm,abkn->arnm", turned, inverse_first[:, :, :, :lower], precision=precise
        )
        return (signal / (first * second)).reshape(2, rows, lower * second)
    signal = jnp.einsum("brkm,bkn->rnm", turned, inverse_first[0][:, :, :lower], precision=precise)
    return (signal / (first * second)).reshape(rows, lower * second)


def complex_product(left, right):
    return jnp.stack(
        [left[0] * right[0] - left[1] * right[1], left[0] * right[1] + left[1] * right[0]]
    )


def conjugate_product(left, right):
    return jnp.stack(
        [left[0] * right[0] + left[1] * right[1], left[0] * right[1] - left[1] * right[0]]
    )


def mirror(array, seq_dim):
    moved = array
    for bit_index in range(lax.axis_size("seq").bit_length() - 1):
        moved = swapped(moved, "seq", bit_index)
    return jnp.flip(moved, axis=seq_dim)


def to_channels(stacked):
    return lax.all_to_all(stacked, "seq", split_axis=1, concat_axis=2, tiled=True)


def to_tokens(stacked):
    return lax.all_to_all(stacked, "seq", split_axis=2, concat_axis=1, tiled=True)


def body(tokens, w_query, w_value, w_out, long_filter, cotangent):
    floats = jnp.float32
    halves = jnp.bfloat16
    half = w_query.shape[0]
    seq_count = lax.axis_size("seq")
    batch_count = lax.axis_size("batch")
    length = tokens.shape[1] * seq_count
    first, second = split_sizes(length)
    tables = make_tables(first, second)
    scale = (2.0 * batch_count * length) ** (-0.5)
    source = tokens[0]
    front = source[:, :half]
    back = source[:, half:]
    back_strand = mirror(back, 0)[:, ::-1]
    strands = jnp.stack([front, back_strand])
    query = jnp.einsum("stk,kh->sht", strands, w_query, preferred_element_type=floats).astype(
        halves
    )
    value = jnp.einsum("stk,kh->sht", strands, w_value, preferred_element_type=floats).astype(
        halves
    )
    value_sig = to_channels(value).astype(floats)
    value_spec = forward_spectrum(value_sig, tables, first, second)
    taps_spec = forward_spectrum(
        jnp.stack([long_filter, jnp.zeros_like(long_filter)]), tables, first, second
    )
    conv_sig = inverse_spectrum(complex_product(value_spec, taps_spec), tables, first, second, True)
    conv_tok = to_tokens(conv_sig.astype(halves))
    gated = (query.astype(floats) * conv_tok.astype(floats)).astype(halves)
    gated_back = mirror(gated[1], 1)
    out_front = jnp.einsum("ht,hk->tk", gated[0], w_out, preferred_element_type=floats)
    out_back = jnp.einsum("ht,hk->tk", gated_back, w_out, preferred_element_type=floats)
    block_out = jnp.concatenate(
        [front.astype(floats) + out_front, back.astype(floats) + out_back[:, ::-1]], axis=1
    ).astype(halves)[None]
    upstream = cotangent[0]
    up_front = upstream[:, :half]
    up_back = upstream[:, half:]
    grad_back = mirror(up_back, 0)[:, ::-1]
    grad_strands = jnp.stack([up_front, grad_back])
    grad_gated = jnp.einsum(
        "stk,hk->sht", grad_strands, w_out, preferred_element_type=floats
    ).astype(halves)
    grad_query_t = (grad_gated.astype(floats) * conv_tok.astype(floats)).astype(halves)
    grad_conv = (grad_gated.astype(floats) * query.astype(floats)).astype(halves)
    grad_sig = to_channels(grad_conv).astype(floats)
    grad_spec = forward_spectrum(grad_sig, tables, first, second)
    value_grad_sig = inverse_spectrum(
        conjugate_product(taps_spec, grad_spec), tables, first, second, True
    )
    filter_part = (
        inverse_spectrum(conjugate_product(value_spec, grad_spec), tables, first, second, False)
        * scale
    )
    grad_value_t = to_tokens(value_grad_sig.astype(halves))
    front_in = jnp.einsum(
        "ht,kh->tk", grad_query_t[0], w_query, preferred_element_type=floats
    ) + jnp.einsum("ht,kh->tk", grad_value_t[0], w_value, preferred_element_type=floats)
    paired = jnp.stack([grad_query_t[1], grad_value_t[1]])
    paired = mirror(paired, 2)
    back_in = jnp.einsum(
        "ht,kh->tk", paired[0], w_query, preferred_element_type=floats
    ) + jnp.einsum("ht,kh->tk", paired[1], w_value, preferred_element_type=floats)
    grad_tokens = jnp.concatenate(
        [up_front.astype(floats) + front_in, up_back.astype(floats) + back_in[:, ::-1]], axis=1
    ).astype(halves)[None]
    term_query = jnp.einsum("stk,sht->kh", strands, grad_query_t, preferred_element_type=floats)
    term_value = jnp.einsum("stk,sht->kh", strands, grad_value_t, preferred_element_type=floats)
    term_out = jnp.einsum("sht,stk->hk", gated, grad_strands, preferred_element_type=floats)
    share = lax.psum_scatter(
        jnp.concatenate([term_query, term_value, term_out], axis=1) * scale,
        "seq",
        scatter_dimension=0,
        tiled=True,
    )
    share, filter_total = (
        lax.psum(share.astype(jnp.bfloat16), "batch").astype(jnp.float32),
        lax.psum(filter_part.astype(jnp.bfloat16), "batch").astype(jnp.float32),
    )
    return (
        block_out,
        grad_tokens,
        share[:, :half],
        share[:, half : 2 * half],
        share[:, 2 * half :],
        filter_total,
    )


def solution(mesh):
    in_specs = (P("batch", "seq", None), P(), P(), P(), P("seq", None), P("batch", "seq", None))
    out_specs = (
        P("batch", "seq", None),
        P("batch", "seq", None),
        P("seq", None),
        P("seq", None),
        P("seq", None),
        P("seq", None),
    )
    return jax.shard_map(body, mesh=mesh, in_specs=in_specs, out_specs=out_specs, check_vma=False)
```

profile of v0, /device:TPU:0, one launch (start us, length us, event | category | flops | bytes accessed | tf_op | source)
XLA Modules:
  0.0 290.6 jit_solution(196216083540338696)
XLA Ops:
  8.2 3.0 %collective-permute-start = (bf16[128,512]{1,0:T(8,128)(2,1)S(1)}, bf16[128,512]{1,0:T(8,128)(2,1)S(1)}, u32[]{:S(2)}, u32[]{:S(2)}) collective-permute-start(bf16[128,512]{1,0:T(8,128)(2,1)S(1)} %get-tuple-element.64), channel_id=1, source_target_pairs={{0,1},{1,0},{2,3},{3,2},{4,5},{5,4},{6,7},{7,6},{8,9},{9,8},{10,11... | collective-permute-start | bytes 393224 | tf_op jit(solution)/shard_map/ppermute | solution.py:11
  12.4 2.8 collective-permute-done
  15.2 2.0 collective-permute-start.1
  17.6 1.8 collective-permute-start.7
  20.8 3.2 %collective-permute-start.2 = (bf16[128,512]{1,0:T(8,128)(2,1)S(1)}, bf16[128,512]{1,0:T(8,128)(2,1)S(1)}, u32[]{:S(2)}, u32[]{:S(2)}) collective-permute-start(bf16[128,512]{1,0:T(8,128)(2,1)S(1)} %collective-permute-done.1), channel_id=1, source_target_pairs={{0,4},{1,5},{2,6},{3,7},{4,0},{5,1},{6,2},{7,3},{8,12},{9,13},{10,... | collective-permute-start | bytes 393224 | tf_op jit(solution)/shard_map/ppermute | solution.py:11
  24.3 2.4 collective-permute-start.8
  26.8 6.2 %collective-permute-done.2 = bf16[128,512]{1,0:T(8,128)(2,1)S(1)} collective-permute-done((bf16[128,512]{1,0:T(8,128)(2,1)S(1)}, bf16[128,512]{1,0:T(8,128)(2,1)S(1)}, u32[]{:S(2)}, u32[]{:S(2)}) %collective-permute-start.2) | collective-permute-done | bytes 131104 | tf_op jit(solution)/shard_map/ppermute | solution.py:11
  37.3 5.2 %all-to-all-start.2 = ((bf16[2,512,128]{2,0,1:T(2,128)(2,1)}), bf16[2,512,128]{2,0,1:T(2,128)(2,1)S(1)}, u32[]{:S(2)}, u32[]{:S(2)}) async-start(bf16[2,512,128]{2,0,1:T(2,128)(2,1)} %copy.140), calls=%async_computation.2 | async-start | bytes 524288 | tf_op jit(solution)/shard_map/all_to_all | solution.py:96
  44.5 6.3 %all-to-all-done.2 = bf16[2,512,128]{2,0,1:T(2,128)(2,1)S(1)} async-done(((bf16[2,512,128]{2,0,1:T(2,128)(2,1)}), bf16[2,512,128]{2,0,1:T(2,128)(2,1)S(1)}, u32[]{:S(2)}, u32[]{:S(2)}) %all-to-all-start.2) | async-done | bytes 262176 | tf_op jit(solution)/shard_map/all_to_all | solution.py:96
  50.8 4.2 %all-to-all-start = ((bf16[2,512,128]{2,0,1:T(2,128)(2,1)}), bf16[2,512,128]{2,0,1:T(2,128)(2,1)}, u32[]{:S(2)}, u32[]{:S(2)}) async-start(bf16[2,512,128]{2,0,1:T(2,128)(2,1)} %copy.122), calls=%async_computation | async-start | bytes 524288 | tf_op jit(solution)/shard_map/all_to_all | solution.py:96
  56.7 1.5 convolution_bitcast_fusion
  58.9 2.0 copy.142
  60.9 3.1 %convolution_bitcast_fusion.1 = f32[2,64,64,32]{1,2,3,0:T(8,128)} fusion(bf16[2,64,32,32]{1,3,2,0:T(8,128)(2,1)} %bitcast.316, f32[1,2,64,64]{3,2,1,0:T(8,128)S(1)} %get-tuple-element.66, f32[1,2,64,64]{3,2,1,0:T(8,128)S(1)} %get-tuple-element.77), kind=kOutput, calls=%fused_computation.41 | convolution fusion | flops 100671488 | bytes 1376256 | tf_op jit(solution)/shard_map/brnm,abnk->arkm/dot_general | solution.py:49
  64.0 1.7 copy.123
  65.7 2.0 copy.124
  67.7 1.9 convolution_bitcast_fusion.2
  69.6 2.6 multiply_add_fusion.4
  72.4 2.7 copy.129
  75.2 1.7 pad_maximum_fusion.3
  76.9 2.7 copy.144
  79.6 2.8 fusion.28
  85.0 2.4 fusion.37
  87.3 3.3 %copy.146 = f32[2,32,64,64]{2,3,1,0:T(8,128)} copy(f32[2,32,64,64]{3,1,2,0:T(8,128)} %fusion.37) | data formatting | bytes 2097152 | tf_op jit(solution)/shard_map/brkj,abjm->arkm/dot_general | solution.py:63
  90.7 3.2 %pad_maximum_fusion = f32[2,64,64,32]{1,2,3,0:T(8,128)} fusion(f32[1,64,64,32]{1,2,3,0:T(8,128)} %get-tuple-element.75, f32[1,64,64,32]{1,2,3,0:T(8,128)} %get-tuple-element.76), kind=kLoop, calls=%fused_computation.1 | loop fusion | flops 262144 | bytes 2097152 | tf_op jit(solution)/shard_map/stack | solution.py:50
  93.9 3.8 %copy.126 = f32[2,64,64,32]{2,3,0,1:T(8,128)} copy(f32[2,64,64,32]{1,2,3,0:T(8,128)} %pad_maximum_fusion) | data formatting | bytes 2097152 | tf_op jit(solution)/shard_map/stack | solution.py:50
  97.7 2.8 fusion.25
  100.5 2.1 multiply_add_fusion.1
  103.7 2.2 copy.131
  105.9 2.6 fusion.40
  108.5 2.3 copy.160
  110.8 4.4 %multiply_subtract_fusion = (f32[1,64,64,32]{1,2,3,0:T(8,128)S(1)}, f32[1,64,64,32]{1,2,3,0:T(8,128)}, f32[1,64,64,32]{1,2,3,0:T(8,128)S(1)}, f32[1,64,64,32]{1,...) fusion(f32[2,64,64,32]{1,2,3,0:T(8,128)} %bitcast.299, f32[64,32]{0,1:T(8,128)S(1)} %get-tuple-element.89, ...), kind=kLoop, calls=%fused_computation.77 | loop fusion | flops 2359296 | bytes 6307840 | tf_op jit(solution)/shard_map/sub | solution.py:65
  117.5 2.1 reshape.296
  119.6 5.7 %all-to-all-start.3 = ((bf16[8,2,8192]{2,1,0:T(2,128)(2,1)}), bf16[8,2,8192]{2,1,0:T(2,128)(2,1)}, u32[]{:S(2)}, u32[]{:S(2)}) async-start(bf16[8,2,8192]{2,1,0:T(2,128)(2,1)} %reshape.296), calls=%async_computation.3 | async-start | bytes 524288 | tf_op jit(solution)/shard_map/all_to_all | solution.py:100
  125.3 1.9 fusion.52
  129.1 4.5 %all-to-all-done.3 = bf16[8,2,8192]{2,1,0:T(2,128)(2,1)} async-done(((bf16[8,2,8192]{2,1,0:T(2,128)(2,1)}), bf16[8,2,8192]{2,1,0:T(2,128)(2,1)}, u32[]{:S(2)}, u32[]{:S(2)}) %all-to-all-start.3) | async-done | bytes 262176 | tf_op jit(solution)/shard_map/all_to_all | solution.py:100
  133.7 4.1 %all-to-all-start.1 = ((bf16[8,2,8192]{2,1,0:T(2,128)(2,1)}), bf16[8,2,8192]{2,1,0:T(2,128)(2,1)}, u32[]{:S(2)}, u32[]{:S(2)}) async-start(bf16[8,2,8192]{2,1,0:T(2,128)(2,1)} %reshape.294), calls=%async_computation.1 | async-start | bytes 524288 | tf_op jit(solution)/shard_map/all_to_all | solution.py:100
  141.1 4.8 %all-to-all-done.1 = bf16[8,2,8192]{2,1,0:T(2,128)(2,1)} async-done(((bf16[8,2,8192]{2,1,0:T(2,128)(2,1)}), bf16[8,2,8192]{2,1,0:T(2,128)(2,1)}, u32[]{:S(2)}, u32[]{:S(2)}) %all-to-all-start.1) | async-done | bytes 262176 | tf_op jit(solution)/shard_map/all_to_all | solution.py:100
  152.2 2.1 maximum_multiply_fusion
  154.3 3.5 %copy.204 = f32[512,1536]{1,0:T(8,128)} copy(f32[512,1536]{0,1:T(8,128)} %maximum_multiply_fusion) | data formatting | bytes 6291456
  158.5 1.9 fusion.65
  161.9 2.1 collective-permute-start.3
  164.3 9.5 %collective-permute-done.3 = bf16[512,128]{0,1:T(8,128)(2,1)S(1)} collective-permute-done((bf16[512,128]{0,1:T(8,128)(2,1)S(1)}, bf16[512,128]{0,1:T(8,128)(2,1)S(1)}, u32[]{:S(2)}, u32[]{:S(2)}) %collective-permute-start.3) | collective-permute-done | bytes 131104 | tf_op jit(solution)/shard_map/ppermute | solution.py:11
  174.2 13.3 %collective-permute-done.4 = bf16[512,128]{0,1:T(8,128)(2,1)S(1)} collective-permute-done((bf16[512,128]{0,1:T(8,128)(2,1)S(1)}, bf16[512,128]{0,1:T(8,128)(2,1)S(1)}, u32[]{:S(2)}, u32[]{:S(2)}) %collective-permute-start.4) | collective-permute-done | bytes 131104 | tf_op jit(solution)/shard_map/ppermute | solution.py:11
  188.0 16.3 %collective-permute-done.5 = bf16[512,128]{0,1:T(8,128)(2,1)S(1)} collective-permute-done((bf16[512,128]{0,1:T(8,128)(2,1)S(1)}, bf16[512,128]{0,1:T(8,128)(2,1)S(1)}, u32[]{:S(2)}, u32[]{:S(2)}) %collective-permute-start.5) | collective-permute-done | bytes 131104 | tf_op jit(solution)/shard_map/ppermute | solution.py:11
  207.0 7.8 %collective-permute-done.11 = bf16[2,512,128]{1,2,0:T(8,128)(2,1)S(1)} collective-permute-done((bf16[2,512,128]{1,2,0:T(8,128)(2,1)S(1)}, bf16[2,512,128]{1,2,0:T(8,128)(2,1)S(1)}, u32[]{:S(2)}, u32[]{:S(2)}) %collective-permute-start.11) | collective-permute-done | bytes 262176 | tf_op jit(solution)/shard_map/ppermute | solution.py:11
  216.3 27.5 %reduce-scatter.4.cloned.1.call-done = f32[64,1536]{1,0:T(8,128)} async-done(((f32[512,1536]{1,0:T(8,128)}), f32[64,1536]{1,0:T(8,128)}) %reduce-scatter.4.cloned.1.call-update) | async-done | bytes 393232
  243.8 1.9 copy.205
  246.5 33.0 %all-reduce.4.cloned.1.call-done = (bf16[64,1536]{0,1:T(8,128)(2,1)}, bf16[64,1024]{0,1:T(8,128)(2,1)}) async-done(((bf16[64,1536]{0,1:T(8,128)(2,1)}, bf16[64,1024]{0,1:T(8,128)(2,1)}), (bf16[64,1536]{0,1:T(8,128)(2,1)}, bf16[64,1024]{0,1:T(8,128)(2,1)})) %all-reduce.4.cloned.1.call-update) | async-done | bytes 327696 | tf_op jit(solution)/shard_map/psum | solution.py:179
  (152 shorter events, 42.7 us)
Async XLA Ops:
  7.2 28.1 %copy-start = (bf16[512,512]{1,0:T(8,128)(2,1)S(1)}, bf16[512,512]{1,0:T(8,128)(2,1)}, u32[]{:S(2)}) copy-start(bf16[512,512]{1,0:T(8,128)(2,1)} %param.9) | copy-start | bytes 1572868
  8.2 131.6 %copy-start.9 = (bf16[1,128,512]{2,1,0:T(8,128)(2,1)}, bf16[1,128,512]{2,1,0:T(8,128)(2,1)S(1)}, u32[]{:S(2)}) copy-start(bf16[1,128,512]{2,1,0:T(8,128)(2,1)S(1)} %get-tuple-element.63) | copy-start | bytes 393220
  8.2 6.9 %collective-permute-start = (bf16[128,512]{1,0:T(8,128)(2,1)S(1)}, bf16[128,512]{1,0:T(8,128)(2,1)S(1)}, u32[]{:S(2)}, u32[]{:S(2)}) collective-permute-start(bf16[128,512]{1,0:T(8,128)(2,1)S(1)} %get-tuple-element.64), channel_id=1, source_target_pairs={{0,1},{1,0},{2,3},{3,2},{4,5},{5,4},{6,7},{7,6},{8,9},{9,8},{10,11... | collective-permute-start | bytes 393224 | tf_op jit(solution)/shard_map/ppermute | solution.py:11
  12.3 25.0 %copy-start.14 = (bf16[1,128,512]{2,1,0:T(8,128)(2,1)}, bf16[1,128,512]{2,1,0:T(8,128)(2,1)S(1)}, u32[]{:S(2)}) copy-start(bf16[1,128,512]{2,1,0:T(8,128)(2,1)S(1)} %get-tuple-element.61) | copy-start | bytes 393220
  12.3 5.3 %collective-permute-start.6 = (bf16[128,512]{1,0:T(8,128)(2,1)S(1)}, bf16[128,512]{1,0:T(8,128)(2,1)S(1)}, u32[]{:S(2)}, u32[]{:S(2)}) collective-permute-start(bf16[128,512]{1,0:T(8,128)(2,1)S(1)} %get-tuple-element.62), channel_id=1, source_target_pairs={{0,1},{1,0},{2,3},{3,2},{4,5},{5,4},{6,7},{7,6},{8,9},{9,8},{10,11... | collective-permute-start | bytes 393224 | tf_op jit(solution)/shard_map/ppermute | solution.py:11
  15.2 5.6 %collective-permute-start.1 = (bf16[128,512]{1,0:T(8,128)(2,1)S(1)}, bf16[128,512]{1,0:T(8,128)(2,1)S(1)}, u32[]{:S(2)}, u32[]{:S(2)}) collective-permute-start(bf16[128,512]{1,0:T(8,128)(2,1)S(1)} %collective-permute-done), channel_id=1, source_target_pairs={{0,2},{1,3},{2,0},{3,1},{4,6},{5,7},{6,4},{7,5},{8,10},{9,11},{10,... | collective-permute-start | bytes 393224 | tf_op jit(solution)/shard_map/ppermute | solution.py:11
  17.3 38.7 %copy-start.25 = (f32[1,64,64]{2,1,0:T(8,128)}, f32[1,64,64]{2,1,0:T(8,128)S(1)}, u32[]{:S(2)}) copy-start(f32[1,64,64]{2,1,0:T(8,128)S(1)} %fusion.120) | copy-start | bytes 49156
  17.6 6.8 %collective-permute-start.7 = (bf16[128,512]{1,0:T(8,128)(2,1)S(1)}, bf16[128,512]{1,0:T(8,128)(2,1)S(1)}, u32[]{:S(2)}, u32[]{:S(2)}) collective-permute-start(bf16[128,512]{1,0:T(8,128)(2,1)S(1)} %collective-permute-done.6), channel_id=1, source_target_pairs={{0,2},{1,3},{2,0},{3,1},{4,6},{5,7},{6,4},{7,5},{8,10},{9,11},{10,... | collective-permute-start | bytes 393224 | tf_op jit(solution)/shard_map/ppermute | solution.py:11
  20.8 12.2 %collective-permute-start.2 = (bf16[128,512]{1,0:T(8,128)(2,1)S(1)}, bf16[128,512]{1,0:T(8,128)(2,1)S(1)}, u32[]{:S(2)}, u32[]{:S(2)}) collective-permute-start(bf16[128,512]{1,0:T(8,128)(2,1)S(1)} %collective-permute-done.1), channel_id=1, source_target_pairs={{0,4},{1,5},{2,6},{3,7},{4,0},{5,1},{6,2},{7,3},{8,12},{9,13},{10,... | collective-permute-start | bytes 393224 | tf_op jit(solution)/shard_map/ppermute | solution.py:11
  24.2 31.8 %copy-start.27 = (f32[1,64,64]{2,1,0:T(8,128)}, f32[1,64,64]{2,1,0:T(8,128)S(1)}, u32[]{:S(2)}) copy-start(f32[1,64,64]{2,1,0:T(8,128)S(1)} %get-tuple-element.87) | copy-start | bytes 49156
  24.3 10.5 %collective-permute-start.8 = (bf16[128,512]{1,0:T(8,128)(2,1)S(1)}, bf16[128,512]{1,0:T(8,128)(2,1)S(1)}, u32[]{:S(2)}, u32[]{:S(2)}) collective-permute-start(bf16[128,512]{1,0:T(8,128)(2,1)S(1)} %collective-permute-done.7), channel_id=1, source_target_pairs={{0,4},{1,5},{2,6},{3,7},{4,0},{5,1},{6,2},{7,3},{8,12},{9,13},{10,... | collective-permute-start | bytes 393224 | tf_op jit(solution)/shard_map/ppermute | solution.py:11
  34.8 8.5 %copy-start.11 = (bf16[512,512]{1,0:T(8,128)(2,1)S(1)}, bf16[512,512]{1,0:T(8,128)(2,1)}, u32[]{:S(2)}) copy-start(bf16[512,512]{1,0:T(8,128)(2,1)} %param.8) | copy-start | bytes 1572868
  35.3 8.3 %copy-start.13 = (bf16[128,512]{1,0:T(8,128)(2,1)}, bf16[128,512]{1,0:T(8,128)(2,1)S(1)}, u32[]{:S(2)}) copy-start(bf16[128,512]{1,0:T(8,128)(2,1)S(1)} %rev.24) | copy-start | bytes 393220
  36.4 19.3 %copy-start.29 = (f32[64,1024]{1,0:T(8,128)S(1)}, f32[64,1024]{1,0:T(8,128)}, u32[]{:S(2)}) copy-start(f32[64,1024]{1,0:T(8,128)} %param.10) | copy-start | bytes 786436
  37.3 13.5 %all-to-all-start.2 = ((bf16[2,512,128]{2,0,1:T(2,128)(2,1)}), bf16[2,512,128]{2,0,1:T(2,128)(2,1)S(1)}, u32[]{:S(2)}, u32[]{:S(2)}) async-start(bf16[2,512,128]{2,0,1:T(2,128)(2,1)} %copy.140), calls=%async_computation.2 | async-start | bytes 524288 | tf_op jit(solution)/shard_map/all_to_all | solution.py:96
  50.8 5.9 %copy-start.17 = (bf16[2,512,128]{2,0,1:T(2,128)(2,1)}, bf16[2,512,128]{2,0,1:T(2,128)(2,1)S(1)}, u32[]{:S(2)}) copy-start(bf16[2,512,128]{2,0,1:T(2,128)(2,1)S(1)} %all-to-all-done.2) | copy-start | bytes 786436
  50.8 13.2 %all-to-all-start = ((bf16[2,512,128]{2,0,1:T(2,128)(2,1)}), bf16[2,512,128]{2,0,1:T(2,128)(2,1)}, u32[]{:S(2)}, u32[]{:S(2)}) async-start(bf16[2,512,128]{2,0,1:T(2,128)(2,1)} %copy.122), calls=%async_computation | async-start | bytes 524288 | tf_op jit(solution)/shard_map/all_to_all | solution.py:96
  56.7 1.5 copy-start.18
  67.7 2.0 copy-start.4
  67.7 2.0 copy-start.31
  76.9 2.8 copy-start.23
  76.9 2.8 copy-start.24
  79.6 2.8 copy-start.3
  83.5 1.4 copy-start.1
  83.6 1.4 copy-start.21
  83.6 1.4 copy-start.22
  97.7 2.8 copy-start.2
  110.8 4.4 %copy-start.19 = (f32[1,2,64,64]{3,2,1,0:T(8,128)S(1)}, f32[1,2,64,64]{3,2,1,0:T(8,128)}, u32[]{:S(2)}) copy-start(f32[1,2,64,64]{3,2,1,0:T(8,128)} %get-tuple-element.65) | copy-start | bytes 98308
  110.8 4.4 %copy-start.20 = (f32[1,2,64,64]{3,2,1,0:T(8,128)S(1)}, f32[1,2,64,64]{3,2,1,0:T(8,128)}, u32[]{:S(2)}) copy-start(f32[1,2,64,64]{3,2,1,0:T(8,128)} %get-tuple-element.78) | copy-start | bytes 98308
  119.6 14.1 %all-to-all-start.3 = ((bf16[8,2,8192]{2,1,0:T(2,128)(2,1)}), bf16[8,2,8192]{2,1,0:T(2,128)(2,1)}, u32[]{:S(2)}, u32[]{:S(2)}) async-start(bf16[8,2,8192]{2,1,0:T(2,128)(2,1)} %reshape.296), calls=%async_computation.3 | async-start | bytes 524288 | tf_op jit(solution)/shard_map/all_to_all | solution.py:100
  133.7 12.3 %all-to-all-start.1 = ((bf16[8,2,8192]{2,1,0:T(2,128)(2,1)}), bf16[8,2,8192]{2,1,0:T(2,128)(2,1)}, u32[]{:S(2)}, u32[]{:S(2)}) async-start(bf16[8,2,8192]{2,1,0:T(2,128)(2,1)} %reshape.294), calls=%async_computation.1 | async-start | bytes 524288 | tf_op jit(solution)/shard_map/all_to_all | solution.py:100
  137.7 106.0 %reduce-scatter.4.cloned.1.call-start = ((), (), s32[]{:S(2)}) async-start(), calls=%async_computation.5 | async-start | bytes 3538944
  148.9 2.9 copy-start.10
  150.4 1.4 copy-start.7
  150.4 1.8 copy-start.6
  157.8 3.7 %copy-start.8 = (bf16[2,512,128]{1,2,0:T(8,128)(2,1)S(1)}, bf16[2,512,128]{1,2,0:T(8,128)(2,1)}, u32[]{:S(2)}) copy-start(bf16[2,512,128]{1,2,0:T(8,128)(2,1)} %copy-done.7) | copy-start | bytes 786436
  157.8 121.7 %all-reduce.4.cloned.1.call-start = ((), (), s32[]{:S(2)}) async-start(), calls=%async_computation.6 | async-start | bytes 1310720 | tf_op jit(solution)/shard_map/psum | solution.py:179
  160.4 3.5 %copy-start.5 = (bf16[512,512]{1,0:T(8,128)(2,1)S(1)}, bf16[512,512]{1,0:T(8,128)(2,1)}, u32[]{:S(2)}) copy-start(bf16[512,512]{1,0:T(8,128)(2,1)} %param.7) | copy-start | bytes 1572868
  161.3 12.6 %copy-start.12 = (bf16[512,512]{1,0:T(8,128)(2,1)S(1)}, bf16[512,512]{1,0:T(8,128)(2,1)}, u32[]{:S(2)}) copy-start(bf16[512,512]{1,0:T(8,128)(2,1)} %param.8) | copy-start | bytes 1572868
  161.3 12.6 %copy-start.16 = (bf16[1,128,1024]{2,1,0:T(8,128)(2,1)S(1)}, bf16[1,128,1024]{2,1,0:T(8,128)(2,1)}, u32[]{:S(2)}) copy-start(bf16[1,128,1024]{2,1,0:T(8,128)(2,1)} %param.11) | copy-start | bytes 786436
  161.6 26.2 %copy-start.15 = (bf16[1,128,1024]{2,1,0:T(8,128)(2,1)S(1)}, bf16[1,128,1024]{2,1,0:T(8,128)(2,1)}, u32[]{:S(2)}) copy-start(bf16[1,128,1024]{2,1,0:T(8,128)(2,1)} %param.6) | copy-start | bytes 786436
  161.8 25.7 %collective-permute-start.9 = (bf16[2,512,128]{1,2,0:T(8,128)(2,1)S(1)}, bf16[2,512,128]{1,2,0:T(8,128)(2,1)}, u32[]{:S(2)}, u32[]{:S(2)}) collective-permute-start(bf16[2,512,128]{1,2,0:T(8,128)(2,1)S(1)} %pad_maximum_fusion.9), channel_id=1, source_target_pairs={{0,1},{1,0},{2,3},{3,2},{4,5},{5,4},{6,7},{7,6},{8,9},{9,8},{10,11... | collective-permute-start | bytes 786440 | tf_op jit(solution)/shard_map/ppermute | solution.py:11
  161.9 11.9 %collective-permute-start.3 = (bf16[512,128]{0,1:T(8,128)(2,1)S(1)}, bf16[512,128]{0,1:T(8,128)(2,1)S(1)}, u32[]{:S(2)}, u32[]{:S(2)}) collective-permute-start(bf16[512,128]{0,1:T(8,128)(2,1)S(1)} %slice_bitcast_fusion.2), channel_id=1, source_target_pairs={{0,1},{1,0},{2,3},{3,2},{4,5},{5,4},{6,7},{7,6},{8,9},{9,8},{10,11... | collective-permute-start | bytes 393224 | tf_op jit(solution)/shard_map/ppermute | solution.py:11
  173.8 13.7 %collective-permute-start.4 = (bf16[512,128]{0,1:T(8,128)(2,1)S(1)}, bf16[512,128]{0,1:T(8,128)(2,1)S(1)}, u32[]{:S(2)}, u32[]{:S(2)}) collective-permute-start(bf16[512,128]{0,1:T(8,128)(2,1)S(1)} %collective-permute-done.3), channel_id=1, source_target_pairs={{0,2},{1,3},{2,0},{3,1},{4,6},{5,7},{6,4},{7,5},{8,10},{9,11},{10,... | collective-permute-start | bytes 393224 | tf_op jit(solution)/shard_map/ppermute | solution.py:11
  187.5 16.7 %collective-permute-start.5 = (bf16[512,128]{0,1:T(8,128)(2,1)S(1)}, bf16[512,128]{0,1:T(8,128)(2,1)S(1)}, u32[]{:S(2)}, u32[]{:S(2)}) collective-permute-start(bf16[512,128]{0,1:T(8,128)(2,1)S(1)} %collective-permute-done.4), channel_id=1, source_target_pairs={{0,4},{1,5},{2,6},{3,7},{4,0},{5,1},{6,2},{7,3},{8,12},{9,13},{10,... | collective-permute-start | bytes 393224 | tf_op jit(solution)/shard_map/ppermute | solution.py:11
  187.5 17.5 %collective-permute-start.10 = (bf16[2,512,128]{1,2,0:T(8,128)(2,1)}, bf16[2,512,128]{1,2,0:T(8,128)(2,1)S(1)}, u32[]{:S(2)}, u32[]{:S(2)}) collective-permute-start(bf16[2,512,128]{1,2,0:T(8,128)(2,1)} %collective-permute-done.9), channel_id=1, source_target_pairs={{0,2},{1,3},{2,0},{3,1},{4,6},{5,7},{6,4},{7,5},{8,10},{9,11},{10,... | collective-permute-start | bytes 786440 | tf_op jit(solution)/shard_map/ppermute | solution.py:11
  205.0 9.8 %collective-permute-start.11 = (bf16[2,512,128]{1,2,0:T(8,128)(2,1)S(1)}, bf16[2,512,128]{1,2,0:T(8,128)(2,1)S(1)}, u32[]{:S(2)}, u32[]{:S(2)}) collective-permute-start(bf16[2,512,128]{1,2,0:T(8,128)(2,1)S(1)} %collective-permute-done.10), channel_id=1, source_target_pairs={{0,4},{1,5},{2,6},{3,7},{4,0},{5,1},{6,2},{7,3},{8,12},{9,13},{10,... | collective-permute-start | bytes 786440 | tf_op jit(solution)/shard_map/ppermute | solution.py:11
  279.5 3.5 %copy-start.30 = (bf16[64,1024]{0,1:T(8,128)(2,1)S(1)}, bf16[64,1024]{0,1:T(8,128)(2,1)}, u32[]{:S(2)}) copy-start(bf16[64,1024]{0,1:T(8,128)(2,1)} %get-tuple-element.31) | copy-start | bytes 393220
  (2 other events, 1.5 us)
Sparse Core Ops, SparseCore 0:
  157.9 85.8 reduce-scatter.3
  246.3 33.2 all-reduce.3
where the time goes:
time: 292 us; the launch traced here: 291 us
  waiting for transfers between devices  134 us (46%)
  local copies, waits for them, and re-layouts  52.8 us (18%)
  starting transfers between devices  35.6 us (12%)
  matrix products  31.2 us (11%)
  other arithmetic  22.3 us (8%)
  between operations  14.8 us (5%)
    ppermute x12, waiting for transfers between devices, swapped(): lax.ppermute(x, axis, [(i, i ^ 1 << stride) for i in range(lax.axis_size(...  57.8 us
    psum x1, waiting for transfers between devices, body(): lax.psum(share.astype(jnp.bfloat16), 'batch').astype(jnp.float32)  33 us
    unnamed x3, waiting for transfers between devices  27.5 us
    unnamed x76, local copies, waits for them, and re-layouts  16.4 us
    ppermute x12, starting transfers between devices, swapped(): lax.ppermute(x, axis, [(i, i ^ 1 << stride) for i in range(lax.axis_size(...  16.2 us
    all_to_all x2, starting transfers between devices, to_tokens(): lax.all_to_all(stacked, 'seq', split_axis=2, concat_axis=1, tiled=True)  9.78 us
    all_to_all x2, starting transfers between devices, to_channels(): lax.all_to_all(stacked, 'seq', split_axis=1, concat_axis=2, tiled=True)  9.47 us
    all_to_all x2, waiting for transfers between devices, to_tokens(): lax.all_to_all(stacked, 'seq', split_axis=2, concat_axis=1, tiled=True)  9.38 us
  transfers between devices with their start and end apart: 18, of which 14 were waited for; matrix products, arithmetic and copies ran while one was open for 10% of the time, Pallas kernels for 0%

commit v1 on v0

--- a/solution.py
+++ b/solution.py
@@ -176,7 +176,7 @@
         tiled=True,
     )
     share, filter_total = (
-        lax.psum(share.astype(jnp.bfloat16), "batch").astype(jnp.float32),
+        jnp.sum(lax.all_gather(share.astype(jnp.bfloat16), "batch"), axis=0).astype(jnp.float32),
         lax.psum(filter_part.astype(jnp.bfloat16), "batch").astype(jnp.float32),
     )
     return (

time: 292 us -> 255 us (0.87)
  waiting for transfers between devices: 134 us -> 84.3 us
  blocking collectives: 0 us -> 8.63 us
  starting transfers between devices: 35.6 us -> 41.1 us
    unnamed x3 -> x2, waiting for transfers between devices: 27.5 us -> 0.03 us
    psum x1, waiting for transfers between devices: 33 us -> 17.4 us  [body(): lax.psum(filter_part.astype(jnp.bfloat16), 'batch').astype(jnp.float32)]
    ppermute x12, waiting for transfers between devices: 57.8 us -> 46.3 us  [swapped(): lax.ppermute(x, axis, [(i, i ^ 1 << stride) for i in range(lax.axis_size(...]
    all_gather x0 -> x1, blocking collectives: none -> 8.63 us  [body(): lax.all_gather(share.astype(jnp.bfloat16), 'batch')]
    reduce_scatter x0 -> x1, waiting for transfers between devices: none -> 7.63 us  [body(): lax.psum_scatter(jnp.concatenate([term_query, term_value, term_out], axis...]
    ppermute x12, starting transfers between devices: 16.2 us -> 21.8 us  [swapped(): lax.ppermute(x, axis, [(i, i ^ 1 << stride) for i in range(lax.axis_size(...]
    unnamed x76 -> x68, local copies, waits for them, and re-layouts: 16.4 us -> 13.5 us
  transfers between devices with their start and end apart: 18 -> 18, of which waited for: 14 -> 15; matrix products, arithmetic and copies ran while one was open for 10% -> 17% of each run, Pallas kernels for 0% -> 0%
where the time goes in v1:
time: 255 us; the launch traced here: 253 us
  waiting for transfers between devices  84.3 us (33%)
  local copies, waits for them, and re-layouts  50.4 us (20%)
  starting transfers between devices  41.1 us (16%)
  matrix products  29.3 us (11%)
  other arithmetic  23.4 us (9%)
  between operations  16.2 us (6%)
  blocking collectives  8.63 us (3%)
    ppermute x12, waiting for transfers between devices, swapped(): lax.ppermute(x, axis, [(i, i ^ 1 << stride) for i in range(lax.axis_size(...  46.3 us
    ppermute x12, starting transfers between devices, swapped(): lax.ppermute(x, axis, [(i, i ^ 1 << stride) for i in range(lax.axis_size(...  21.8 us
    psum x1, waiting for transfers between devices, body(): lax.psum(filter_part.astype(jnp.bfloat16), 'batch').astype(jnp.float32)  17.4 us
    unnamed x68, local copies, waits for them, and re-layouts  13.5 us
    all_to_all x2, starting transfers between devices, to_tokens(): lax.all_to_all(stacked, 'seq', split_axis=2, concat_axis=1, tiled=True)  9.76 us
    all_to_all x2, starting transfers between devices, to_channels(): lax.all_to_all(stacked, 'seq', split_axis=1, concat_axis=2, tiled=True)  9.46 us
    another operation x3, local copies, waits for them, and re-layouts, forward_spectrum(): jnp.stack([section[0] * cos_twist + section[1] * sin_twist, section[1] *...  9.36 us
    all_gather x1, blocking collectives, body(): lax.all_gather(share.astype(jnp.bfloat16), 'batch')  8.63 us
  transfers between devices with their start and end apart: 18, of which 15 were waited for; matrix products, arithmetic and copies ran while one was open for 17% of the time, Pallas kernels for 0%

profile of v1, /device:TPU:0, one launch (start us, length us, event | category | flops | bytes accessed | tf_op | source)
XLA Modules:
  0.0 253.3 jit_solution(7137198861297130004)
XLA Ops:
  9.1 3.0 %collective-permute-start = (bf16[128,512]{1,0:T(8,128)(2,1)S(1)}, bf16[128,512]{1,0:T(8,128)(2,1)S(1)}, u32[]{:S(2)}, u32[]{:S(2)}) collective-permute-start(bf16[128,512]{1,0:T(8,128)(2,1)S(1)} %get-tuple-element.53), channel_id=1, source_target_pairs={{0,1},{1,0},{2,3},{3,2},{4,5},{5,4},{6,7},{7,6},{8,9},{9,8},{10,11... | collective-permute-start | bytes 393224 | tf_op jit(solution)/shard_map/ppermute | solution.py:11
  13.2 2.8 %collective-permute-done = bf16[128,512]{1,0:T(8,128)(2,1)S(1)} collective-permute-done((bf16[128,512]{1,0:T(8,128)(2,1)S(1)}, bf16[128,512]{1,0:T(8,128)(2,1)S(1)}, u32[]{:S(2)}, u32[]{:S(2)}) %collective-permute-start) | collective-permute-done | bytes 131104 | tf_op jit(solution)/shard_map/ppermute | solution.py:11
  16.0 2.0 collective-permute-start.1
  18.4 1.8 collective-permute-start.7
  21.6 3.2 %collective-permute-start.2 = (bf16[128,512]{1,0:T(8,128)(2,1)S(1)}, bf16[128,512]{1,0:T(8,128)(2,1)S(1)}, u32[]{:S(2)}, u32[]{:S(2)}) collective-permute-start(bf16[128,512]{1,0:T(8,128)(2,1)S(1)} %collective-permute-done.1), channel_id=1, source_target_pairs={{0,4},{1,5},{2,6},{3,7},{4,0},{5,1},{6,2},{7,3},{8,12},{9,13},{10,... | collective-permute-start | bytes 393224 | tf_op jit(solution)/shard_map/ppermute | solution.py:11
  25.2 2.4 collective-permute-start.8
  27.6 6.2 %collective-permute-done.2 = bf16[128,512]{1,0:T(8,128)(2,1)S(1)} collective-permute-done((bf16[128,512]{1,0:T(8,128)(2,1)S(1)}, bf16[128,512]{1,0:T(8,128)(2,1)S(1)}, u32[]{:S(2)}, u32[]{:S(2)}) %collective-permute-start.2) | collective-permute-done | bytes 131104 | tf_op jit(solution)/shard_map/ppermute | solution.py:11
  38.1 5.2 %all-to-all-start.2 = ((bf16[2,512,128]{2,0,1:T(2,128)(2,1)}), bf16[2,512,128]{2,0,1:T(2,128)(2,1)S(1)}, u32[]{:S(2)}, u32[]{:S(2)}) async-start(bf16[2,512,128]{2,0,1:T(2,128)(2,1)} %copy.133), calls=%async_computation.2 | async-start | bytes 524288 | tf_op jit(solution)/shard_map/all_to_all | solution.py:96
  45.3 6.3 %all-to-all-done.2 = bf16[2,512,128]{2,0,1:T(2,128)(2,1)S(1)} async-done(((bf16[2,512,128]{2,0,1:T(2,128)(2,1)}), bf16[2,512,128]{2,0,1:T(2,128)(2,1)S(1)}, u32[]{:S(2)}, u32[]{:S(2)}) %all-to-all-start.2) | async-done | bytes 262176 | tf_op jit(solution)/shard_map/all_to_all | solution.py:96
  51.6 4.2 %all-to-all-start = ((bf16[2,512,128]{2,0,1:T(2,128)(2,1)}), bf16[2,512,128]{2,0,1:T(2,128)(2,1)}, u32[]{:S(2)}, u32[]{:S(2)}) async-start(bf16[2,512,128]{2,0,1:T(2,128)(2,1)} %copy.115), calls=%async_computation | async-start | bytes 524288 | tf_op jit(solution)/shard_map/all_to_all | solution.py:96
  59.7 1.9 copy.135
  61.7 3.2 %convolution_bitcast_fusion.1 = f32[2,64,64,32]{1,2,3,0:T(8,128)} fusion(bf16[2,64,32,32]{1,3,2,0:T(8,128)(2,1)} %bitcast.318, f32[1,2,64,64]{3,2,1,0:T(8,128)S(1)} %get-tuple-element.58, f32[1,2,64,64]{3,2,1,0:T(8,128)S(1)} %get-tuple-element.69), kind=kOutput, calls=%fused_computation.41 | convolution fusion | flops 100671488 | bytes 1376256 | tf_op jit(solution)/shard_map/brnm,abnk->arkm/dot_general | solution.py:49
  66.5 1.9 copy.117
  68.5 1.9 convolution_bitcast_fusion.2
  70.5 2.6 %multiply_add_fusion.4 = (f32[1,64,64,32]{1,2,3,0:T(8,128)}, f32[1,64,64,32]{1,2,3,0:T(8,128)}, f32[1,64,64,32]{1,2,3,0:T(8,128)S(1)}, f32[1,64,64,32]{1,2,3,0:T...) fusion(f32[2,64,64,32]{1,2,3,0:T(8,128)S(1)} %copy-done.4, f32[64,32]{0,1:T(8,128)S(1)} %get-tuple-element.81, ...), kind=kLoop, calls=%fused_computation.85 | loop fusion | flops 2359296 | bytes 6307840 | tf_op jit(solution)/shard_map/add | solution.py:52
  73.3 2.8 %copy.122 = f32[2,64,64,32]{2,3,0,1:T(8,128)} copy(f32[2,64,64,32]{1,2,3,0:T(8,128)S(1)} %pad_maximum_fusion.1) | data formatting | bytes 2097152 | tf_op jit(solution)/shard_map/stack | solution.py:50
  77.8 2.8 %copy.137 = f32[2,64,64,32]{2,3,0,1:T(8,128)} copy(f32[2,64,64,32]{1,2,3,0:T(8,128)S(1)} %pad_maximum_fusion.3) | data formatting | bytes 2097152 | tf_op jit(solution)/shard_map/stack | solution.py:50
  80.5 2.8 %fusion.28 = f32[2,64,64,32]{2,3,1,0:T(8,128)S(1)} fusion(f32[2,64,64,32]{2,3,0,1:T(8,128)} %copy.122, f32[1,2,32,32]{2,3,1,0:T(8,128)S(1)} %copy-done.22, f32[1,2,32,32]{2,3,1,0:T(8,128)S(1)} %copy-done.23), kind=kOutput, calls=%fused_computation.35 | convolution fusion | flops 100667392 | bytes 2113536 | tf_op jit(solution)/shard_map/brkm,abmj->arkj/dot_general | solution.py:56
  85.8 2.4 fusion.37
  88.2 3.3 %copy.139 = f32[2,32,64,64]{2,3,1,0:T(8,128)} copy(f32[2,32,64,64]{3,1,2,0:T(8,128)} %fusion.37) | data formatting | bytes 2097152 | tf_op jit(solution)/shard_map/brkj,abjm->arkm/dot_general | solution.py:63
  91.6 3.2 %pad_maximum_fusion = f32[2,64,64,32]{1,2,3,0:T(8,128)} fusion(f32[1,64,64,32]{1,2,3,0:T(8,128)} %get-tuple-element.67, f32[1,64,64,32]{1,2,3,0:T(8,128)} %get-tuple-element.68), kind=kLoop, calls=%fused_computation.1 | loop fusion | flops 262144 | bytes 2097152 | tf_op jit(solution)/shard_map/stack | solution.py:50
  94.7 3.8 %copy.119 = f32[2,64,64,32]{2,3,0,1:T(8,128)} copy(f32[2,64,64,32]{1,2,3,0:T(8,128)} %pad_maximum_fusion) | data formatting | bytes 2097152 | tf_op jit(solution)/shard_map/stack | solution.py:50
  98.6 2.8 %fusion.25 = f32[2,64,64,32]{2,3,1,0:T(8,128)S(1)} fusion(f32[2,64,64,32]{2,3,0,1:T(8,128)} %copy.119, f32[1,2,32,32]{2,3,1,0:T(8,128)S(1)} %copy-done.22, f32[1,2,32,32]{2,3,1,0:T(8,128)S(1)} %copy-done.23), kind=kOutput, calls=%fused_computation.34 | convolution fusion | flops 100667392 | bytes 2113536 | tf_op jit(solution)/shard_map/brkm,abmj->arkj/dot_general | solution.py:56
  101.4 2.2 multiply_add_fusion.1
  104.6 2.2 copy.124
  106.8 2.6 %fusion.40 = f32[2,32,64,64]{3,1,2,0:T(8,128)S(1)} fusion(f32[1,2,32,32]{2,3,1,0:T(8,128)S(1)} %copy-done.21, f32[1,2,32,32]{2,3,1,0:T(8,128)S(1)} %copy-done.20, f32[1,64,64,32]{2,3,1,0:T(8,128)} %get-tuple-element.25, f32[1,64,64,32]{2,3,1,0:T(8,128)} %get-tuple-element.24), kind=kOutput, calls=%fused_computation.39 | convolution fusion | flops 100929536 | bytes 2113536 | tf_op jit(solution)/shard_map/brkj,abjm->arkm/dot_general | solution.py:63
  109.4 2.3 copy.154
  111.6 4.4 %multiply_subtract_fusion = (f32[1,64,64,32]{1,2,3,0:T(8,128)S(1)}, f32[1,64,64,32]{1,2,3,0:T(8,128)S(1)}, f32[1,64,64,32]{1,2,3,0:T(8,128)}, f32[1,64,64,32]{1,...) fusion(f32[2,64,64,32]{1,2,3,0:T(8,128)} %bitcast.300, f32[64,32]{0,1:T(8,128)S(1)} %get-tuple-element.81, ...), kind=kLoop, calls=%fused_computation.77 | loop fusion | flops 2359296 | bytes 6307840 | tf_op jit(solution)/shard_map/sub | solution.py:65
  118.4 2.1 reshape.297
  120.5 5.7 %all-to-all-start.3 = ((bf16[8,2,8192]{2,1,0:T(2,128)(2,1)}), bf16[8,2,8192]{2,1,0:T(2,128)(2,1)}, u32[]{:S(2)}, u32[]{:S(2)}) async-start(bf16[8,2,8192]{2,1,0:T(2,128)(2,1)} %reshape.297), calls=%async_computation.3 | async-start | bytes 524288 | tf_op jit(solution)/shard_map/all_to_all | solution.py:100
  126.2 2.2 fusion.52
  130.1 2.1 reshape.295
  132.2 2.4 all-to-all-done.3
  134.6 4.0 %all-to-all-start.1 = ((bf16[8,2,8192]{2,1,0:T(2,128)(2,1)}), bf16[8,2,8192]{2,1,0:T(2,128)(2,1)}, u32[]{:S(2)}, u32[]{:S(2)}) async-start(bf16[8,2,8192]{2,1,0:T(2,128)(2,1)} %reshape.295), calls=%async_computation.1 | async-start | bytes 524288 | tf_op jit(solution)/shard_map/all_to_all | solution.py:100
  142.6 4.3 %all-to-all-done.1 = bf16[8,2,8192]{2,1,0:T(2,128)(2,1)} async-done(((bf16[8,2,8192]{2,1,0:T(2,128)(2,1)}), bf16[8,2,8192]{2,1,0:T(2,128)(2,1)}, u32[]{:S(2)}, u32[]{:S(2)}) %all-to-all-start.1) | async-done | bytes 262176 | tf_op jit(solution)/shard_map/all_to_all | solution.py:100
  153.0 2.1 maximum_multiply_fusion
  155.1 3.5 %copy.195 = f32[512,1536]{1,0:T(8,128)} copy(f32[512,1536]{0,1:T(8,128)} %maximum_multiply_fusion) | data formatting | bytes 6291456
  158.6 17.4 %all-reduce.3.cloned.1.call-done = bf16[64,1024]{0,1:T(8,128)(2,1)} async-done(((bf16[64,1024]{0,1:T(8,128)(2,1)}), bf16[64,1024]{0,1:T(8,128)(2,1)}) %all-reduce.3.cloned.1.call-update) | async-done | bytes 131088 | tf_op jit(solution)/shard_map/psum | solution.py:180
  176.0 1.8 copy.158
  180.8 11.3 %collective-permute-done.3 = bf16[512,128]{0,1:T(8,128)(2,1)S(1)} collective-permute-done((bf16[512,128]{0,1:T(8,128)(2,1)S(1)}, bf16[512,128]{0,1:T(8,128)(2,1)S(1)}, u32[]{:S(2)}, u32[]{:S(2)}) %collective-permute-start.3) | collective-permute-done | bytes 131104 | tf_op jit(solution)/shard_map/ppermute | solution.py:11
  192.1 2.1 collective-permute-start.4
  194.5 2.6 %collective-permute-done.4 = bf16[512,128]{0,1:T(8,128)(2,1)S(1)} collective-permute-done((bf16[512,128]{0,1:T(8,128)(2,1)S(1)}, bf16[512,128]{0,1:T(8,128)(2,1)S(1)}, u32[]{:S(2)}, u32[]{:S(2)}) %collective-permute-start.4) | collective-permute-done | bytes 131104 | tf_op jit(solution)/shard_map/ppermute | solution.py:11
  197.1 3.0 %collective-permute-start.5 = (bf16[512,128]{0,1:T(8,128)(2,1)S(1)}, bf16[512,128]{0,1:T(8,128)(2,1)S(1)}, u32[]{:S(2)}, u32[]{:S(2)}) collective-permute-start(bf16[512,128]{0,1:T(8,128)(2,1)S(1)} %collective-permute-done.4), channel_id=1, source_target_pairs={{0,4},{1,5},{2,6},{3,7},{4,0},{5,1},{6,2},{7,3},{8,12},{9,13},{10,... | collective-permute-start | bytes 393224 | tf_op jit(solution)/shard_map/ppermute | solution.py:11
  201.3 2.9 %collective-permute-done.5 = bf16[512,128]{0,1:T(8,128)(2,1)S(1)} collective-permute-done((bf16[512,128]{0,1:T(8,128)(2,1)S(1)}, bf16[512,128]{0,1:T(8,128)(2,1)S(1)}, u32[]{:S(2)}, u32[]{:S(2)}) %collective-permute-start.5) | collective-permute-done | bytes 131104 | tf_op jit(solution)/shard_map/ppermute | solution.py:11
  205.0 3.3 %collective-permute-done.10 = bf16[2,512,128]{1,2,0:T(8,128)(2,1)S(1)} collective-permute-done((bf16[2,512,128]{1,2,0:T(8,128)(2,1)}, bf16[2,512,128]{1,2,0:T(8,128)(2,1)S(1)}, u32[]{:S(2)}, u32[]{:S(2)}) %collective-permute-start.10) | collective-permute-done | bytes 262176 | tf_op jit(solution)/shard_map/ppermute | solution.py:11
  210.2 15.3 %collective-permute-done.11 = bf16[2,512,128]{1,2,0:T(8,128)(2,1)S(1)} collective-permute-done((bf16[2,512,128]{1,2,0:T(8,128)(2,1)S(1)}, bf16[2,512,128]{1,2,0:T(8,128)(2,1)S(1)}, u32[]{:S(2)}, u32[]{:S(2)}) %collective-permute-start.11) | collective-permute-done | bytes 262176 | tf_op jit(solution)/shard_map/ppermute | solution.py:11
  227.7 7.6 %reduce-scatter.4.cloned.1.call-done = f32[64,1536]{1,0:T(8,128)} async-done(((f32[512,1536]{1,0:T(8,128)}), f32[64,1536]{1,0:T(8,128)}) %reduce-scatter.4.cloned.1.call-update) | async-done | bytes 393232 | tf_op jit(solution)/shard_map/reduce_scatter | solution.py:172
  236.3 8.6 %all-gather = bf16[256,1536]{1,0:T(8,128)(2,1)S(1)} all-gather(bf16[64,1536]{1,0:T(8,128)(2,1)S(1)} %convert_element_type.266), channel_id=2, replica_groups=mesh['batch'=4,'seq'=8] {'batch'}, dimensions={0}, use_global_device_ids=true | all-gather | bytes 983040 | tf_op jit(solution)/shard_map/all_gather | solution.py:179
  (147 shorter events, 46.5 us)
Async XLA Ops:
  8.0 28.1 %copy-start = (bf16[512,512]{1,0:T(8,128)(2,1)S(1)}, bf16[512,512]{1,0:T(8,128)(2,1)}, u32[]{:S(2)}) copy-start(bf16[512,512]{1,0:T(8,128)(2,1)} %param.9) | copy-start | bytes 1572868
  9.1 133.2 %copy-start.8 = (bf16[1,128,512]{2,1,0:T(8,128)(2,1)}, bf16[1,128,512]{2,1,0:T(8,128)(2,1)S(1)}, u32[]{:S(2)}) copy-start(bf16[1,128,512]{2,1,0:T(8,128)(2,1)S(1)} %get-tuple-element.52) | copy-start | bytes 393220
  9.1 6.9 %collective-permute-start = (bf16[128,512]{1,0:T(8,128)(2,1)S(1)}, bf16[128,512]{1,0:T(8,128)(2,1)S(1)}, u32[]{:S(2)}, u32[]{:S(2)}) collective-permute-start(bf16[128,512]{1,0:T(8,128)(2,1)S(1)} %get-tuple-element.53), channel_id=1, source_target_pairs={{0,1},{1,0},{2,3},{3,2},{4,5},{5,4},{6,7},{7,6},{8,9},{9,8},{10,11... | collective-permute-start | bytes 393224 | tf_op jit(solution)/shard_map/ppermute | solution.py:11
  13.1 25.0 %copy-start.13 = (bf16[1,128,512]{2,1,0:T(8,128)(2,1)}, bf16[1,128,512]{2,1,0:T(8,128)(2,1)S(1)}, u32[]{:S(2)}) copy-start(bf16[1,128,512]{2,1,0:T(8,128)(2,1)S(1)} %get-tuple-element.50) | copy-start | bytes 393220
  13.1 5.3 %collective-permute-start.6 = (bf16[128,512]{1,0:T(8,128)(2,1)S(1)}, bf16[128,512]{1,0:T(8,128)(2,1)S(1)}, u32[]{:S(2)}, u32[]{:S(2)}) collective-permute-start(bf16[128,512]{1,0:T(8,128)(2,1)S(1)} %get-tuple-element.51), channel_id=1, source_target_pairs={{0,1},{1,0},{2,3},{3,2},{4,5},{5,4},{6,7},{7,6},{8,9},{9,8},{10,11... | collective-permute-start | bytes 393224 | tf_op jit(solution)/shard_map/ppermute | solution.py:11
  16.0 5.6 %collective-permute-start.1 = (bf16[128,512]{1,0:T(8,128)(2,1)S(1)}, bf16[128,512]{1,0:T(8,128)(2,1)S(1)}, u32[]{:S(2)}, u32[]{:S(2)}) collective-permute-start(bf16[128,512]{1,0:T(8,128)(2,1)S(1)} %collective-permute-done), channel_id=1, source_target_pairs={{0,2},{1,3},{2,0},{3,1},{4,6},{5,7},{6,4},{7,5},{8,10},{9,11},{10,... | collective-permute-start | bytes 393224 | tf_op jit(solution)/shard_map/ppermute | solution.py:11
  18.1 38.7 %copy-start.24 = (f32[1,64,64]{2,1,0:T(8,128)}, f32[1,64,64]{2,1,0:T(8,128)S(1)}, u32[]{:S(2)}) copy-start(f32[1,64,64]{2,1,0:T(8,128)S(1)} %fusion.120) | copy-start | bytes 49156
  18.4 6.8 %collective-permute-start.7 = (bf16[128,512]{1,0:T(8,128)(2,1)S(1)}, bf16[128,512]{1,0:T(8,128)(2,1)S(1)}, u32[]{:S(2)}, u32[]{:S(2)}) collective-permute-start(bf16[128,512]{1,0:T(8,128)(2,1)S(1)} %collective-permute-done.6), channel_id=1, source_target_pairs={{0,2},{1,3},{2,0},{3,1},{4,6},{5,7},{6,4},{7,5},{8,10},{9,11},{10,... | collective-permute-start | bytes 393224 | tf_op jit(solution)/shard_map/ppermute | solution.py:11
  21.6 12.2 %collective-permute-start.2 = (bf16[128,512]{1,0:T(8,128)(2,1)S(1)}, bf16[128,512]{1,0:T(8,128)(2,1)S(1)}, u32[]{:S(2)}, u32[]{:S(2)}) collective-permute-start(bf16[128,512]{1,0:T(8,128)(2,1)S(1)} %collective-permute-done.1), channel_id=1, source_target_pairs={{0,4},{1,5},{2,6},{3,7},{4,0},{5,1},{6,2},{7,3},{8,12},{9,13},{10,... | collective-permute-start | bytes 393224 | tf_op jit(solution)/shard_map/ppermute | solution.py:11
  25.0 31.8 %copy-start.26 = (f32[1,64,64]{2,1,0:T(8,128)}, f32[1,64,64]{2,1,0:T(8,128)S(1)}, u32[]{:S(2)}) copy-start(f32[1,64,64]{2,1,0:T(8,128)S(1)} %get-tuple-element.79) | copy-start | bytes 49156
  25.2 10.5 %collective-permute-start.8 = (bf16[128,512]{1,0:T(8,128)(2,1)S(1)}, bf16[128,512]{1,0:T(8,128)(2,1)S(1)}, u32[]{:S(2)}, u32[]{:S(2)}) collective-permute-start(bf16[128,512]{1,0:T(8,128)(2,1)S(1)} %collective-permute-done.7), channel_id=1, source_target_pairs={{0,4},{1,5},{2,6},{3,7},{4,0},{5,1},{6,2},{7,3},{8,12},{9,13},{10,... | collective-permute-start | bytes 393224 | tf_op jit(solution)/shard_map/ppermute | solution.py:11
  35.6 8.5 %copy-start.10 = (bf16[512,512]{1,0:T(8,128)(2,1)S(1)}, bf16[512,512]{1,0:T(8,128)(2,1)}, u32[]{:S(2)}) copy-start(bf16[512,512]{1,0:T(8,128)(2,1)} %param.8) | copy-start | bytes 1572868
  36.1 8.3 %copy-start.12 = (bf16[128,512]{1,0:T(8,128)(2,1)}, bf16[128,512]{1,0:T(8,128)(2,1)S(1)}, u32[]{:S(2)}) copy-start(bf16[128,512]{1,0:T(8,128)(2,1)S(1)} %rev.24) | copy-start | bytes 393220
  37.3 19.3 %copy-start.28 = (f32[64,1024]{1,0:T(8,128)S(1)}, f32[64,1024]{1,0:T(8,128)}, u32[]{:S(2)}) copy-start(f32[64,1024]{1,0:T(8,128)} %param.10) | copy-start | bytes 786436
  38.1 13.5 %all-to-all-start.2 = ((bf16[2,512,128]{2,0,1:T(2,128)(2,1)}), bf16[2,512,128]{2,0,1:T(2,128)(2,1)S(1)}, u32[]{:S(2)}, u32[]{:S(2)}) async-start(bf16[2,512,128]{2,0,1:T(2,128)(2,1)} %copy.133), calls=%async_computation.2 | async-start | bytes 524288 | tf_op jit(solution)/shard_map/all_to_all | solution.py:96
  51.6 5.9 %copy-start.16 = (bf16[2,512,128]{2,0,1:T(2,128)(2,1)}, bf16[2,512,128]{2,0,1:T(2,128)(2,1)S(1)}, u32[]{:S(2)}) copy-start(bf16[2,512,128]{2,0,1:T(2,128)(2,1)S(1)} %all-to-all-done.2) | copy-start | bytes 786436
  51.6 13.2 %all-to-all-start = ((bf16[2,512,128]{2,0,1:T(2,128)(2,1)}), bf16[2,512,128]{2,0,1:T(2,128)(2,1)}, u32[]{:S(2)}, u32[]{:S(2)}) async-start(bf16[2,512,128]{2,0,1:T(2,128)(2,1)} %copy.115), calls=%async_computation | async-start | bytes 524288 | tf_op jit(solution)/shard_map/all_to_all | solution.py:96
  57.5 1.5 copy-start.17
  68.5 2.0 copy-start.4
  68.5 2.0 copy-start.29
  77.7 2.8 %copy-start.22 = (f32[1,2,32,32]{2,3,1,0:T(8,128)S(1)}, f32[1,2,32,32]{2,3,1,0:T(8,128)}, u32[]{:S(2)}) copy-start(f32[1,2,32,32]{2,3,1,0:T(8,128)} %get-tuple-element.72) | copy-start | bytes 24580
  77.8 2.8 %copy-start.23 = (f32[1,2,32,32]{2,3,1,0:T(8,128)S(1)}, f32[1,2,32,32]{2,3,1,0:T(8,128)}, u32[]{:S(2)}) copy-start(f32[1,2,32,32]{2,3,1,0:T(8,128)} %get-tuple-element.75) | copy-start | bytes 24580
  80.5 2.8 %copy-start.3 = (f32[2,64,64,32]{2,3,0,1:T(8,128)S(1)}, f32[2,64,64,32]{2,3,0,1:T(8,128)}, u32[]{:S(2)}) copy-start(f32[2,64,64,32]{2,3,0,1:T(8,128)} %copy.137) | copy-start | bytes 3145732
  84.4 1.4 copy-start.1
  84.4 1.4 copy-start.20
  84.4 1.4 copy-start.21
  98.6 2.8 %copy-start.2 = (f32[2,64,64,32]{2,3,1,0:T(8,128)S(1)}, f32[2,64,64,32]{2,3,1,0:T(8,128)}, u32[]{:S(2)}) copy-start(f32[2,64,64,32]{2,3,1,0:T(8,128)} %copy-done.1) | copy-start | bytes 3145732
  111.6 4.4 %copy-start.18 = (f32[1,2,64,64]{3,2,1,0:T(8,128)S(1)}, f32[1,2,64,64]{3,2,1,0:T(8,128)}, u32[]{:S(2)}) copy-start(f32[1,2,64,64]{3,2,1,0:T(8,128)} %get-tuple-element.57) | copy-start | bytes 98308
  111.6 4.4 %copy-start.19 = (f32[1,2,64,64]{3,2,1,0:T(8,128)S(1)}, f32[1,2,64,64]{3,2,1,0:T(8,128)}, u32[]{:S(2)}) copy-start(f32[1,2,64,64]{3,2,1,0:T(8,128)} %get-tuple-element.70) | copy-start | bytes 98308
  120.5 14.1 %all-to-all-start.3 = ((bf16[8,2,8192]{2,1,0:T(2,128)(2,1)}), bf16[8,2,8192]{2,1,0:T(2,128)(2,1)}, u32[]{:S(2)}, u32[]{:S(2)}) async-start(bf16[8,2,8192]{2,1,0:T(2,128)(2,1)} %reshape.297), calls=%async_computation.3 | async-start | bytes 524288 | tf_op jit(solution)/shard_map/all_to_all | solution.py:100
  128.5 10.2 %copy-start.25 = (f32[1,64,64]{2,1,0:T(8,128)S(1)}, f32[1,64,64]{2,1,0:T(8,128)}, u32[]{:S(2)}) copy-start(f32[1,64,64]{2,1,0:T(8,128)} %copy-done.24) | copy-start | bytes 49156
  128.5 10.2 %copy-start.27 = (f32[1,64,64]{2,1,0:T(8,128)S(1)}, f32[1,64,64]{2,1,0:T(8,128)}, u32[]{:S(2)}) copy-start(f32[1,64,64]{2,1,0:T(8,128)} %copy-done.26) | copy-start | bytes 49156
  134.6 12.3 %all-to-all-start.1 = ((bf16[8,2,8192]{2,1,0:T(2,128)(2,1)}), bf16[8,2,8192]{2,1,0:T(2,128)(2,1)}, u32[]{:S(2)}, u32[]{:S(2)}) async-start(bf16[8,2,8192]{2,1,0:T(2,128)(2,1)} %reshape.295), calls=%async_computation.1 | async-start | bytes 524288 | tf_op jit(solution)/shard_map/all_to_all | solution.py:100
  138.6 37.4 %all-reduce.3.cloned.1.call-start = ((), (), s32[]{:S(2)}) async-start(), calls=%async_computation.5 | async-start | bytes 524288 | tf_op jit(solution)/shard_map/psum | solution.py:180
  140.2 95.1 %reduce-scatter.4.cloned.1.call-start = ((), (), s32[]{:S(2)}) async-start(), calls=%async_computation.6 | async-start | bytes 3538944 | tf_op jit(solution)/shard_map/reduce_scatter | solution.py:172
  149.8 2.9 %copy-start.9 = (bf16[1,128,512]{2,1,0:T(8,128)(2,1)S(1)}, bf16[1,128,512]{2,1,0:T(8,128)(2,1)}, u32[]{:S(2)}) copy-start(bf16[1,128,512]{2,1,0:T(8,128)(2,1)} %copy-done.8) | copy-start | bytes 393220
  151.2 1.4 copy-start.6
  158.6 19.5 %copy-start.7 = (bf16[2,512,128]{1,2,0:T(8,128)(2,1)S(1)}, bf16[2,512,128]{1,2,0:T(8,128)(2,1)}, u32[]{:S(2)}) copy-start(bf16[2,512,128]{1,2,0:T(8,128)(2,1)} %copy-done.6) | copy-start | bytes 786436
  158.6 21.9 %copy-start.5 = (bf16[512,512]{1,0:T(8,128)(2,1)S(1)}, bf16[512,512]{1,0:T(8,128)(2,1)}, u32[]{:S(2)}) copy-start(bf16[512,512]{1,0:T(8,128)(2,1)} %param.7) | copy-start | bytes 1572868
  177.8 16.4 %copy-start.11 = (bf16[512,512]{1,0:T(8,128)(2,1)S(1)}, bf16[512,512]{1,0:T(8,128)(2,1)}, u32[]{:S(2)}) copy-start(bf16[512,512]{1,0:T(8,128)(2,1)} %param.8) | copy-start | bytes 1572868
  177.8 16.4 %copy-start.15 = (bf16[1,128,1024]{2,1,0:T(8,128)(2,1)S(1)}, bf16[1,128,1024]{2,1,0:T(8,128)(2,1)}, u32[]{:S(2)}) copy-start(bf16[1,128,1024]{2,1,0:T(8,128)(2,1)} %param.11) | copy-start | bytes 786436
  178.1 23.0 %copy-start.14 = (bf16[1,128,1024]{2,1,0:T(8,128)(2,1)S(1)}, bf16[1,128,1024]{2,1,0:T(8,128)(2,1)}, u32[]{:S(2)}) copy-start(bf16[1,128,1024]{2,1,0:T(8,128)(2,1)} %param.6) | copy-start | bytes 786436
  178.3 21.8 %collective-permute-start.9 = (bf16[2,512,128]{1,2,0:T(8,128)(2,1)S(1)}, bf16[2,512,128]{1,2,0:T(8,128)(2,1)}, u32[]{:S(2)}, u32[]{:S(2)}) collective-permute-start(bf16[2,512,128]{1,2,0:T(8,128)(2,1)S(1)} %pad_maximum_fusion.9), channel_id=1, source_target_pairs={{0,1},{1,0},{2,3},{3,2},{4,5},{5,4},{6,7},{7,6},{8,9},{9,8},{10,11... | collective-permute-start | bytes 786440 | tf_op jit(solution)/shard_map/ppermute | solution.py:11
  179.9 12.2 %collective-permute-start.3 = (bf16[512,128]{0,1:T(8,128)(2,1)S(1)}, bf16[512,128]{0,1:T(8,128)(2,1)S(1)}, u32[]{:S(2)}, u32[]{:S(2)}) collective-permute-start(bf16[512,128]{0,1:T(8,128)(2,1)S(1)} %slice_bitcast_fusion.2), channel_id=1, source_target_pairs={{0,1},{1,0},{2,3},{3,2},{4,5},{5,4},{6,7},{7,6},{8,9},{9,8},{10,11... | collective-permute-start | bytes 393224 | tf_op jit(solution)/shard_map/ppermute | solution.py:11
  192.1 5.0 %collective-permute-start.4 = (bf16[512,128]{0,1:T(8,128)(2,1)S(1)}, bf16[512,128]{0,1:T(8,128)(2,1)S(1)}, u32[]{:S(2)}, u32[]{:S(2)}) collective-permute-start(bf16[512,128]{0,1:T(8,128)(2,1)S(1)} %collective-permute-done.3), channel_id=1, source_target_pairs={{0,2},{1,3},{2,0},{3,1},{4,6},{5,7},{6,4},{7,5},{8,10},{9,11},{10,... | collective-permute-start | bytes 393224 | tf_op jit(solution)/shard_map/ppermute | solution.py:11
  197.1 7.1 %collective-permute-start.5 = (bf16[512,128]{0,1:T(8,128)(2,1)S(1)}, bf16[512,128]{0,1:T(8,128)(2,1)S(1)}, u32[]{:S(2)}, u32[]{:S(2)}) collective-permute-start(bf16[512,128]{0,1:T(8,128)(2,1)S(1)} %collective-permute-done.4), channel_id=1, source_target_pairs={{0,4},{1,5},{2,6},{3,7},{4,0},{5,1},{6,2},{7,3},{8,12},{9,13},{10,... | collective-permute-start | bytes 393224 | tf_op jit(solution)/shard_map/ppermute | solution.py:11
  200.1 8.2 %collective-permute-start.10 = (bf16[2,512,128]{1,2,0:T(8,128)(2,1)}, bf16[2,512,128]{1,2,0:T(8,128)(2,1)S(1)}, u32[]{:S(2)}, u32[]{:S(2)}) collective-permute-start(bf16[2,512,128]{1,2,0:T(8,128)(2,1)} %collective-permute-done.9), channel_id=1, source_target_pairs={{0,2},{1,3},{2,0},{3,1},{4,6},{5,7},{6,4},{7,5},{8,10},{9,11},{10,... | collective-permute-start | bytes 786440 | tf_op jit(solution)/shard_map/ppermute | solution.py:11
  208.3 17.2 %collective-permute-start.11 = (bf16[2,512,128]{1,2,0:T(8,128)(2,1)S(1)}, bf16[2,512,128]{1,2,0:T(8,128)(2,1)S(1)}, u32[]{:S(2)}, u32[]{:S(2)}) collective-permute-start(bf16[2,512,128]{1,2,0:T(8,128)(2,1)S(1)} %collective-permute-done.10), channel_id=1, source_target_pairs={{0,4},{1,5},{2,6},{3,7},{4,0},{5,1},{6,2},{7,3},{8,12},{9,13},{10,... | collective-permute-start | bytes 786440 | tf_op jit(solution)/shard_map/ppermute | solution.py:11
Sparse Core Ops, SparseCore 0:
  142.3 33.6 all-reduce.2
Sparse Core Ops, SparseCore 1:
  158.7 76.6 reduce-scatter.3
